TPU v7x, 512 devices: a whole 4x8x8 slice. The times are simulated.
512 devices in a mesh: ctx: 64 (over x, y, core), tp: 8 (over z).
Axes of the slice: x: 4, y: 8, z: 8, core: 2. Of those that a mesh axis runs over, the one named last changes fastest.
Arguments:
- queries: bfloat16 [32768, 2048], P('ctx', 'tp'), may hold values from -1.75 to 1.75
- keys: bfloat16 [32768, 2048], P('ctx', 'tp'), may hold values from -1.75 to 1.75
- values: bfloat16 [32768, 2048], P('ctx', 'tp'), may hold values from -18 to 18
- gain: bfloat16 [2048], P('tp'), may hold values from 0.099609375 to 1.8984375
- cotangent: bfloat16 [32768, 2048], P('ctx', 'tp'), may hold values from -6 to 6
Outputs:
- normed: bfloat16 [32768, 2048], P('ctx', 'tp')
- grad_queries: bfloat16 [32768, 2048], P('ctx', 'tp')
- grad_keys: bfloat16 [32768, 2048], P('ctx', 'tp')
- grad_values: bfloat16 [32768, 2048], P('ctx', 'tp')
All inputs are finite; a program needn't handle non-finite values.
Results may differ from a plain program's by a relative error of at most 0.0058.
Values sent between devices are 32-bit elements; how exact they have to be, the bound alone decides.
A program may use at most 64 MiB of HBM per device.

v0:
```python
import jax
import jax.numpy as jnp
from jax import lax
from jax.sharding import PartitionSpec as P

HEAD = 128
HEADS = 16


epsilon = 1e-06


def heads_first(matrix, head_count):
    return matrix.reshape(matrix.shape[0], head_count, HEAD).transpose(1, 0, 2)


def heads_last(tensor):
    return tensor.transpose(1, 0, 2).reshape(tensor.shape[1], -1)


def shards(queries, keys, values, gain, cotangent):
    row_count = queries.shape[0]
    head_count = queries.shape[1] // HEAD
    query_heads = heads_first(queries, head_count)
    key_heads = heads_first(keys, head_count)
    value_heads = heads_first(values, head_count)
    causal = jnp.tril(jnp.ones((row_count, row_count), jnp.bool_))
    gain_wide = gain.astype(jnp.float32)
    own_state = jnp.einsum(
        "hte,htf->hef", key_heads, value_heads, preferred_element_type=jnp.float32
    )
    position = lax.axis_index("ctx")
    pieces = lax.all_gather(own_state[None], "ctx", axis=0, tiled=True)
    shard_index = jnp.arange(pieces.shape[0], dtype=jnp.int32)
    lower_mask = (shard_index < position).astype(jnp.float32)
    prior_state = jnp.sum(pieces * lower_mask[:, None, None, None], axis=0)
    prior_low = prior_state.astype(jnp.bfloat16)

    def forward_head(members):
        query_now, key_now, value_now, prior_now = members
        scores = jnp.einsum("te,se->ts", query_now, key_now, preferred_element_type=jnp.float32)
        masked = jnp.where(causal, scores, 0.0).astype(jnp.bfloat16)
        combined = jnp.dot(masked, value_now, preferred_element_type=jnp.float32)
        combined = combined + jnp.dot(query_now, prior_now, preferred_element_type=jnp.float32)
        return (masked, combined)

    masked, combined = lax.map(forward_head, (query_heads, key_heads, value_heads, prior_low))
    attended = heads_last(combined)
    scaled = cotangent.astype(jnp.float32) * gain_wide
    totals = lax.psum(
        (jnp.sum(attended * attended, axis=-1), jnp.sum(scaled * attended, axis=-1)), "tp"
    )
    feature_count = HEADS * HEAD
    inverse = lax.rsqrt(totals[0] / feature_count + epsilon)
    mean_product = totals[1] / feature_count
    normed = (attended * inverse[:, None] * gain_wide).astype(jnp.bfloat16)
    grad_att = (
        inverse[:, None] * scaled - (inverse**3 * mean_product)[:, None] * attended
    ).astype(jnp.bfloat16)
    grad_heads = heads_first(grad_att, head_count)

    def middle_head(members):
        query_now, key_now, value_now, grad_now, prior_now = members
        products = jnp.einsum("te,se->ts", grad_now, value_now, preferred_element_type=jnp.float32)
        cross_low = jnp.where(causal, products, 0.0).astype(jnp.bfloat16)
        grad_query = jnp.dot(cross_low, key_now, preferred_element_type=jnp.float32)
        grad_query = grad_query + jnp.einsum(
            "tf,ef->te", grad_now, prior_now, preferred_element_type=jnp.float32
        )
        later_own = jnp.einsum("te,tf->ef", query_now, grad_now, preferred_element_type=jnp.float32)
        return (cross_low, grad_query.astype(jnp.bfloat16), later_own)

    cross_low, grad_query, later_own = lax.map(
        middle_head, (query_heads, key_heads, value_heads, grad_heads, prior_low)
    )
    position_now = lax.axis_index("ctx")
    pieces = lax.all_gather(later_own[None], "ctx", axis=0, tiled=True)
    shard_index = jnp.arange(pieces.shape[0], dtype=jnp.int32)
    upper_mask = (shard_index > position_now).astype(jnp.float32)
    after_state = jnp.sum(pieces * upper_mask[:, None, None, None], axis=0)
    after_low = after_state.astype(jnp.bfloat16)

    def final_head(members):
        query_now, key_now, value_now, grad_now, masked_now, cross_now, after_now = members
        grad_key = jnp.einsum("st,se->te", cross_now, query_now, preferred_element_type=jnp.float32)
        grad_key = grad_key + jnp.einsum(
            "tf,ef->te", value_now, after_now, preferred_element_type=jnp.float32
        )
        grad_value = jnp.einsum(
            "st,sf->tf", masked_now, grad_now, preferred_element_type=jnp.float32
        )
        grad_value = grad_value + jnp.dot(key_now, after_now, preferred_element_type=jnp.float32)
        return (grad_key.astype(jnp.bfloat16), grad_value.astype(jnp.bfloat16))

    grad_key, grad_value = lax.map(
        final_head, (query_heads, key_heads, value_heads, grad_heads, masked, cross_low, after_low)
    )
    return (normed, heads_last(grad_query), heads_last(grad_key), heads_last(grad_value))


def solution(mesh):
    in_specs = (P("ctx", "tp"), P("ctx", "tp"), P("ctx", "tp"), P("tp"), P("ctx", "tp"))
    out_specs = (P("ctx", "tp"), P("ctx", "tp"), P("ctx", "tp"), P("ctx", "tp"))
    return jax.shard_map(shards, mesh=mesh, in_specs=in_specs, out_specs=out_specs, check_vma=False)
```

profile of v0, /device:TPU:1, one launch (start us, length us, event | category | flops | bytes accessed | tf_op | source)
XLA Modules:
  0.0 234.4 jit_solution(15956539192981530037)
XLA Ops:
  7.2 0.0 all-gather.5.cloned.1.call-start
  7.2 1.1 copy.34
  8.3 1.1 copy.35
  9.4 0.9 fusion.81
  10.3 0.0 all-gather.7.cloned.1.call-start
  10.4 0.2 copy.38
  10.5 0.2 copy.39
  10.8 1.1 copy.33
  11.8 0.2 copy.37
  12.0 0.7 convert_element_type.49
  12.7 93.3 %all-gather.5.cloned.1.call-done = f32[128,128,128]{2,1,0:T(8,128)} async-done(((f32[2,128,128]{2,1,0:T(8,128)}), f32[128,128,128]{2,1,0:T(8,128)}) %all-gather.5.cloned.1.call-update) | async-done | bytes 8388624 | tf_op jit(solution)/shard_map/all_gather | solution.py:33
  106.0 4.1 %multiply_reduce_fusion.1 = bf16[2,128,128]{2,1,0:T(8,128)(2,1)S(1)} fusion(f32[64,2,128,128]{3,2,1,0:T(8,128)} %bitcast.213, f32[64]{0:T(128)S(1)} %compare_convert_fusion.1), kind=kLoop, calls=%fused_computation.83 | loop fusion | flops 4161536 | bytes 8454400 | tf_op jit(solution)/shard_map/reduce_sum | solution.py:36
  110.1 0.1 broadcast.22.clone
  110.2 1.6 while.41
  110.2 0.3 bitcast_dynamic-update-slice_fusion.4
  110.5 0.3 fusion.134
  110.8 0.2 fusion.135
  111.0 0.3 bitcast_dynamic-update-slice_fusion.4
  111.3 0.3 fusion.134
  111.6 0.2 fusion.135
  111.8 0.1 fusion.78
  112.0 0.1 fusion.75
  112.2 14.4 %all-reduce = (f32[512]{0:T(512)S(1)}, f32[512]{0:T(512)S(1)}) all-reduce(f32[512]{0:T(512)S(1)} %fusion.78, f32[512]{0:T(512)S(1)} %fusion.75), channel_id=1, replica_groups=mesh['ctx'=64,'tp'=8] {'tp'}, use_global_device_ids=true, to_apply=%region_4.5 | all-reduce | flops 1024 | bytes 8192 | tf_op jit(solution)/shard_map/psum | solution.py:50
  126.6 0.9 fusion.79
  127.5 0.1 broadcast.22
  127.6 3.4 %while.42 = (s32[]{:T(128)}, bf16[2,512,512]{2,1,0:T(8,128)(2,1)S(1)}, bf16[2,512,128]{2,1,0:T(8,128)(2,1)S(1)}, f32[2,128,128]{2,1,0:T(8,128)}, bf16[2,512,128]...) while((s32[]{:T(128)}, ...), condition=%wide.region_8.9_spmd.clone, body=%wide.region_7.8_spmd.clone.sunk | while | flops 168689664 | bytes 3117673 | solution.py:73
  127.6 0.3 bitcast_dynamic-update-slice_fusion.5
  128.0 0.3 fusion.142
  128.3 0.2 fusion.143
  128.5 0.9 fusion.144
  129.3 0.3 bitcast_dynamic-update-slice_fusion.5
  129.7 0.3 fusion.142
  130.0 0.2 fusion.143
  130.2 0.9 fusion.144
  131.1 0.7 copy_bitcast_fusion.2
  131.8 85.6 %all-gather.7.cloned.1.call-done = f32[128,128,128]{2,1,0:T(8,128)} async-done(((f32[2,128,128]{2,1,0:T(8,128)}), f32[128,128,128]{2,1,0:T(8,128)}) %all-gather.7.cloned.1.call-update) | async-done | bytes 8388624 | tf_op jit(solution)/shard_map/all_gather | solution.py:77
  217.5 4.1 %multiply_reduce_fusion = bf16[2,128,128]{2,1,0:T(8,128)(2,1)S(1)} fusion(f32[64,2,128,128]{3,2,1,0:T(8,128)} %bitcast.214, f32[64]{0:T(128)S(1)} %compare_convert_fusion), kind=kLoop, calls=%fused_computation.82 | loop fusion | flops 4161536 | bytes 8454400 | tf_op jit(solution)/shard_map/reduce_sum | solution.py:80
  221.6 0.7 broadcast.24.clone.1
  222.3 3.4 %while.40 = (s32[]{:T(128)}, bf16[2,512,128]{2,1,0:T(8,128)(2,1)S(1)}, bf16[2,512,128]{2,1,0:T(8,128)(2,1)}, bf16[2,512,512]{2,1,0:T(8,128)(2,1)S(1)}, bf16[2,51...) while((s32[]{:T(128)}, ...), condition=%wide.region_11.12_spmd, body=%wide.region_10.11_spmd.sunk | while | flops 168034304 | bytes 2954349 | solution.py:95
  222.3 0.3 fusion.126
  222.7 0.2 fusion.127
  222.9 0.3 fusion.128
  223.2 0.8 fusion.129
  224.1 0.3 fusion.126
  224.4 0.2 fusion.127
  224.6 0.3 fusion.128
  225.0 0.8 fusion.129
  225.8 1.8 copy_bitcast_fusion
  (12 shorter events, 0.2 us)
Async XLA Ops:
  7.2 98.8 %all-gather.5.cloned.1.call-start = ((), (), s32[]{:S(2)}) async-start(), calls=%async_computation | async-start | bytes 8519680 | tf_op jit(solution)/shard_map/all_gather | solution.py:33
  10.3 207.1 %all-gather.7.cloned.1.call-start = ((), (), s32[]{:S(2)}) async-start(), calls=%async_computation.1 | async-start | bytes 8519680 | tf_op jit(solution)/shard_map/all_gather | solution.py:77
  110.1 1.9 copy-start
Sparse Core Ops, SparseCore 0:
  11.9 94.0 all-gather.4
  131.2 86.2 all-gather.6
where the time goes:
time: 235 us; the launch traced here: 234 us
  waiting for transfers between devices  179 us (76%)
  blocking collectives  14.4 us (6%)
  between operations  14.2 us (6%)
  other arithmetic  10.1 us (4%)
  matrix products  9.23 us (4%)
  local copies, waits for them, and re-layouts  7.28 us (3%)
    all_gather x1, waiting for transfers between devices, shards(): pieces = lax.all_gather(own_state[None], 'ctx', axis=0, tiled=True)  93.3 us
    all_gather x1, waiting for transfers between devices, shards(): pieces = lax.all_gather(later_own[None], 'ctx', axis=0, tiled=True)  85.6 us
    psum x1, blocking collectives, shards(): lax.psum((jnp.sum(attended * attended, axis=-1), jnp.sum(scaled * attende...  14.4 us
  transfers between devices with their start and end apart: 2, of which 2 were waited for; matrix products, arithmetic and copies ran while one was open for 1% of the time, Pallas kernels for 0%

commit v1 on v0

v1 whole, which is shorter than its diff:
```python
import jax
import jax.numpy as jnp
from jax import lax
from jax.experimental import pallas as pl
from jax.experimental.pallas import tpu as pltpu
from jax.sharding import PartitionSpec as P

HEAD = 128
HEADS = 16
D = HEAD * HEADS
ROW = 16
COLS = 4
TP = 8
T = 512
H = T // 2
W = 256
PIECE = 16
epsilon = 1e-06
F32 = jnp.float32
BF16 = jnp.bfloat16
MESH = pl.DeviceIdType.MESH

ROW_ORDER = (8, 7, 9, 6, 10, 5, 11, 4, 12, 3, 13, 2, 14, 1, 15)
COL_ORDER = (2, 1, 3)
TP_ORDER = (4, 3, 5, 2, 6, 1, 7)


def dot(a, b, ca, cb):
    return lax.dot_general(a, b, (((ca,), (cb,)), ((), ())), preferred_element_type=F32)


def kernel(
    q_in, k_in, v_in, gain_ref, c_in, n_out, dq_out, dk_out, dv_out,
    q, k, v, c, scaled, att, grad, m_top, m_low, x_top, x_low, dk_acc, dv_acc,
    n_buf, dq_buf, dk_buf, dv_buf, prior_bd, after_bd, stats,
    own_a, gath_a, tot_a, back_a, full_a, own_b, gath_b, tot_b, back_b, full_b,
    in_sem, out_sem, row_send_a, row_recv_a, col_send_a, col_recv_a, ret_send_a, ret_recv_a,
    row_send_b, row_recv_b, col_send_b, col_recv_b, ret_send_b, ret_recv_b, tp_send, tp_recv,
):
    me = lax.axis_index("ctx")
    z = lax.axis_index("tp")
    x = me // ROW
    r = me % ROW

    loads = [
        pltpu.make_async_copy(src, dst, in_sem.at[i])
        for i, (src, dst) in enumerate(((k_in, k), (v_in, v), (q_in, q), (c_in, c)))
    ]
    for load in loads:
        load.start()

    def row_peer(off):
        j = (r + off) % ROW
        return j, (x * ROW + j, z)

    def col_peer(off):
        return (((x + off) % COLS) * ROW + r, z)

    def tp_peer(off):
        return (me, (z + off) % TP)

    barrier = pltpu.get_barrier_semaphore()
    for off in ROW_ORDER:
        pl.semaphore_signal(barrier, inc=1, device_id=row_peer(off)[1], device_id_type=MESH)
    for off in COL_ORDER:
        pl.semaphore_signal(barrier, inc=1, device_id=col_peer(off), device_id_type=MESH)
    for off in TP_ORDER:
        pl.semaphore_signal(barrier, inc=1, device_id=tp_peer(off), device_id_type=MESH)

    prior_bd[...] = jnp.zeros_like(prior_bd)
    after_bd[...] = jnp.zeros_like(after_bd)

    def put_own(own, left, right):
        state = dot(left, right, 0, 0)
        own[0:HEAD, :] = state[0:HEAD, 0:HEAD]
        own[HEAD:W, :] = state[HEAD:W, HEAD:W]

    def row_copies(own, gath, send, recv):
        copies = []
        for off in ROW_ORDER:
            j, peer = row_peer(off)
            copies.append(
                pltpu.make_async_remote_copy(
                    src_ref=own.at[pl.ds(pl.multiple_of(j * PIECE, PIECE), PIECE)],
                    dst_ref=gath.at[r],
                    send_sem=send.at[off],
                    recv_sem=recv.at[off],
                    device_id=peer,
                    device_id_type=MESH,
                )
            )
        return copies

    def col_copies(tot, send, recv):
        return [
            pltpu.make_async_remote_copy(
                src_ref=tot.at[x],
                dst_ref=tot.at[x],
                send_sem=send.at[off],
                recv_sem=recv.at[off],
                device_id=col_peer(off),
                device_id_type=MESH,
            )
            for off in COL_ORDER
        ]

    def ret_copies(back, full, send, recv):
        copies = []
        for off in ROW_ORDER:
            j, peer = row_peer(off)
            copies.append(
                pltpu.make_async_remote_copy(
                    src_ref=back.at[j],
                    dst_ref=full.at[r],
                    send_sem=send.at[off],
                    recv_sem=recv.at[off],
                    device_id=peer,
                    device_id_type=MESH,
                )
            )
        return copies

    def start(copies):
        for copy in copies:
            copy.start()

    def received(copies):
        for copy in copies:
            copy.wait_recv()

    def sent(copies):
        for copy in copies:
            copy.wait_send()

    def scan_row(own, gath, tot, reverse):
        gath[r] = own[pl.ds(pl.multiple_of(r * PIECE, PIECE), PIECE), :]
        run = jnp.zeros((PIECE, HEAD), F32)
        before = [None] * ROW
        for j in reversed(range(ROW)) if reverse else range(ROW):
            before[j] = run
            run = run + gath[j]
        tot[x] = run
        return before

    def scan_back(before, tot, back, full, reverse):
        base = jnp.zeros((PIECE, HEAD), F32)
        for other in range(COLS):
            counts = (other > x) if reverse else (other < x)
            base = base + jnp.where(counts, tot[other], 0.0)
        for j in range(ROW):
            back[j] = before[j] + base

    loads[0].wait()
    loads[1].wait()
    put_own(own_a, k[...], v[...])
    pl.semaphore_wait(barrier, len(ROW_ORDER) + len(COL_ORDER) + len(TP_ORDER))
    row_a = row_copies(own_a, gath_a, row_send_a, row_recv_a)
    start(row_a)

    loads[2].wait()
    loads[3].wait()
    lower = lax.broadcasted_iota(jnp.int32, (H, H), 0) >= lax.broadcasted_iota(jnp.int32, (H, H), 1)

    def masked_products(left, right, top, low):
        for h in range(2):
            cols = slice(h * HEAD, (h + 1) * HEAD)
            top[h] = jnp.where(lower, dot(left[0:H, cols], right[0:H, cols], 1, 1), 0.0).astype(BF16)
            low[h, :, 0:H] = dot(left[H:T, cols], right[0:H, cols], 1, 1).astype(BF16)
            low[h, :, H:T] = jnp.where(
                lower, dot(left[H:T, cols], right[H:T, cols], 1, 1), 0.0
            ).astype(BF16)

    masked_products(q, k, m_top, m_low)
    for h in range(2):
        cols = slice(h * HEAD, (h + 1) * HEAD)
        att[0:H, cols] = dot(m_top[h], v[0:H, cols], 1, 0)
        att[H:T, cols] = dot(m_low[h], v[:, cols], 1, 0)
    gain = gain_ref[...].astype(F32)
    scaled[...] = c[...].astype(F32) * gain

    received(row_a)
    before = scan_row(own_a, gath_a, tot_a, False)
    col_a = col_copies(tot_a, col_send_a, col_recv_a)
    start(col_a)
    received(col_a)
    scan_back(before, tot_a, back_a, full_a, False)
    ret_a = ret_copies(back_a, full_a, ret_send_a, ret_recv_a)
    start(ret_a)
    full_a[r] = back_a[r]
    received(ret_a)

    def put_bd(bd, full):
        low_state = full[...].reshape(W, HEAD).astype(BF16)
        bd[0:HEAD, 0:HEAD] = low_state[0:HEAD]
        bd[HEAD:W, HEAD:W] = low_state[HEAD:W]

    put_bd(prior_bd, full_a)
    att[...] += dot(q[...], prior_bd[...], 1, 0)

    eye = lax.broadcasted_iota(jnp.int32, (HEAD, HEAD), 0) == lax.broadcasted_iota(
        jnp.int32, (HEAD, HEAD), 1
    )
    rows = []
    for kind in range(2):
        for a in range(T // HEAD):
            part = att[a * HEAD:(a + 1) * HEAD, :]
            other = part if kind == 0 else scaled[a * HEAD:(a + 1) * HEAD, :]
            product = part * other
            sums = jnp.sum(product[:, 0:HEAD] + product[:, HEAD:W], axis=1, keepdims=True)
            rows.append(jnp.sum(jnp.where(eye, sums, 0.0), axis=0, keepdims=True))
    stats[z] = jnp.concatenate(rows, axis=0)
    tp_copies = [
        pltpu.make_async_remote_copy(
            src_ref=stats.at[z],
            dst_ref=stats.at[z],
            send_sem=tp_send.at[off],
            recv_sem=tp_recv.at[off],
            device_id=tp_peer(off),
            device_id_type=MESH,
        )
        for off in TP_ORDER
    ]
    start(tp_copies)
    received(tp_copies)
    totals = jnp.sum(stats[...], axis=0)
    inverse_row = lax.rsqrt(totals[0:4] / D + epsilon)
    coef_row = inverse_row * inverse_row * inverse_row * (totals[4:8] / D)

    def column(row):
        return jnp.sum(jnp.where(eye, row, 0.0), axis=1, keepdims=True)

    inverse = []
    for a in range(T // HEAD):
        span = slice(a * HEAD, (a + 1) * HEAD)
        inverse.append(column(inverse_row[a:a + 1]))
        coef = column(coef_row[a:a + 1])
        grad[span, :] = (inverse[a] * scaled[span, :] - coef * att[span, :]).astype(BF16)

    put_own(own_b, q[...], grad[...])
    row_b = row_copies(own_b, gath_b, row_send_b, row_recv_b)
    start(row_b)

    for a in range(T // HEAD):
        span = slice(a * HEAD, (a + 1) * HEAD)
        n_buf[span, :] = (att[span, :] * inverse[a] * gain).astype(BF16)
    stores = [pltpu.make_async_copy(n_buf, n_out, out_sem.at[0])]
    stores[0].start()
    masked_products(grad, v, x_top, x_low)

    received(row_b)
    before = scan_row(own_b, gath_b, tot_b, True)
    col_b = col_copies(tot_b, col_send_b, col_recv_b)
    start(col_b)
    for h in range(2):
        cols = slice(h * HEAD, (h + 1) * HEAD)
        dk_acc[0:H, cols] = dot(x_top[h], q[0:H, cols], 0, 0) + dot(x_low[h, :, 0:H], q[H:T, cols], 0, 0)
        dk_acc[H:T, cols] = dot(x_low[h, :, H:T], q[H:T, cols], 0, 0)
    received(col_b)
    scan_back(before, tot_b, back_b, full_b, True)
    ret_b = ret_copies(back_b, full_b, ret_send_b, ret_recv_b)
    start(ret_b)
    full_b[r] = back_b[r]

    for h in range(2):
        cols = slice(h * HEAD, (h + 1) * HEAD)
        dv_acc[0:H, cols] = dot(m_top[h], grad[0:H, cols], 0, 0) + dot(
            m_low[h, :, 0:H], grad[H:T, cols], 0, 0
        )
        dv_acc[H:T, cols] = dot(m_low[h, :, H:T], grad[H:T, cols], 0, 0)
    for h in range(2):
        cols = slice(h * HEAD, (h + 1) * HEAD)
        from_prior = dot(grad[:, cols], prior_bd[cols, cols], 1, 1)
        dq_buf[0:H, cols] = (dot(x_top[h], k[0:H, cols], 1, 0) + from_prior[0:H]).astype(BF16)
        dq_buf[H:T, cols] = (dot(x_low[h], k[:, cols], 1, 0) + from_prior[H:T]).astype(BF16)
    stores.append(pltpu.make_async_copy(dq_buf, dq_out, out_sem.at[1]))
    stores[1].start()
    for copies in (row_a, col_a, ret_a, tp_copies, row_b, col_b):
        sent(copies)

    received(ret_b)
    put_bd(after_bd, full_b)
    dk_buf[...] = (dk_acc[...] + dot(v[...], after_bd[...], 1, 1)).astype(BF16)
    stores.append(pltpu.make_async_copy(dk_buf, dk_out, out_sem.at[2]))
    stores[2].start()
    dv_buf[...] = (dv_acc[...] + dot(k[...], after_bd[...], 1, 0)).astype(BF16)
    stores.append(pltpu.make_async_copy(dv_buf, dv_out, out_sem.at[3]))
    stores[3].start()
    sent(ret_b)
    for store in stores:
        store.wait()


def shards(queries, keys, values, gain, cotangent):
    block = jax.ShapeDtypeStruct((T, W), BF16)
    anywhere = pl.BlockSpec(memory_space=pl.ANY)
    low = pltpu.VMEM((T, W), BF16)
    wide = pltpu.VMEM((T, W), F32)
    dma = pltpu.SemaphoreType.DMA
    scan_buffers = [
        pltpu.VMEM((W, HEAD), F32),
        pltpu.VMEM((ROW, PIECE, HEAD), F32),
        pltpu.VMEM((COLS, PIECE, HEAD), F32),
        pltpu.VMEM((ROW, PIECE, HEAD), F32),
        pltpu.VMEM((ROW, PIECE, HEAD), F32),
    ]
    scan_sems = [dma((ROW,)), dma((ROW,)), dma((COLS,)), dma((COLS,)), dma((ROW,)), dma((ROW,))]
    top = pltpu.VMEM((2, H, H), BF16)
    bottom = pltpu.VMEM((2, H, T), BF16)
    square = pltpu.VMEM((W, W), BF16)
    return pl.pallas_call(
        kernel,
        out_shape=(block,) * 4,
        in_specs=[anywhere, anywhere, anywhere, pl.BlockSpec(memory_space=pltpu.VMEM), anywhere],
        out_specs=(anywhere,) * 4,
        scratch_shapes=[low, low, low, low, wide, wide, low, top, bottom, top, bottom, wide, wide]
        + [low] * 4
        + [square, square, pltpu.VMEM((TP, 8, HEAD), F32)]
        + scan_buffers
        + scan_buffers
        + [dma((4,)), dma((4,))]
        + scan_sems
        + scan_sems
        + [dma((TP,)), dma((TP,))],
        compiler_params=pltpu.CompilerParams(
            collective_id=0, has_side_effects=True, vmem_limit_bytes=40 * 1024 * 1024
        ),
    )(queries, keys, values, gain.reshape(1, W), cotangent)


def solution(mesh):
    in_specs = (P("ctx", "tp"), P("ctx", "tp"), P("ctx", "tp"), P("tp"), P("ctx", "tp"))
    out_specs = (P("ctx", "tp"), P("ctx", "tp"), P("ctx", "tp"), P("ctx", "tp"))
    return jax.shard_map(shards, mesh=mesh, in_specs=in_specs, out_specs=out_specs, check_vma=False)
```

time: 235 us -> 57.3 us (0.24)
  waiting for transfers between devices: 179 us -> 0 us
  Pallas kernels: 0 us -> 49.2 us
  blocking collectives: 14.4 us -> 0 us
  between operations: 14.2 us -> 0.64 us
  other arithmetic: 10.1 us -> 0 us
  matrix products: 9.23 us -> 0 us
    all_gather x2 -> x0, waiting for transfers between devices: 179 us -> none  [the longest x1 93.3 us: shards(): pieces = lax.all_gather(own_state[None], 'ctx', axis=0, tiled=True)]
    pallas_call x0 -> x1, Pallas kernels: none -> 49.2 us  [shards(): pl.pallas_call(kernel, out_shape=(block,) * 4, in_specs=[anywhere, anywhe...]
    psum x1 -> x0, blocking collectives: 14.4 us -> none  [shards(): lax.psum((jnp.sum(attended * attended, axis=-1), jnp.sum(scaled * attende...]
    dot_general x23 -> x0, matrix products: 9.23 us -> none  [the longest x2 1.73 us: middle_head(): jnp.einsum('te,tf->ef', query_now, grad_now, preferred_element_type=jnp.f...]
    reduce_sum x4 -> x0, other arithmetic: 8.49 us -> none  [the longest x1 4.1 us: shards(): prior_state = jnp.sum(pieces * lower_mask[:, None, None, None], axis=0)]
    unnamed x8 -> x12, local copies, waits for them, and re-layouts: 3.79 us -> 6.61 us
  transfers between devices with their start and end apart: 2 -> 0, of which waited for: 2 -> 0; matrix products, arithmetic and copies ran while one was open for 1% -> 0% of each run, Pallas kernels for 0% -> 0%
where the time goes in v1:
time: 57.3 us; the launch traced here: 57.1 us
  Pallas kernels  49.2 us (86%)
  local copies, waits for them, and re-layouts  7.27 us (13%)
  between operations  0.64 us (1%)
    pallas_call x1, Pallas kernels, shards(): pl.pallas_call(kernel, out_shape=(block,) * 4, in_specs=[anywhere, anywhe...  49.2 us
    unnamed x12, local copies, waits for them, and re-layouts  6.61 us

profile of v1, /device:TPU:1, one launch (start us, length us, event | category | flops | bytes accessed | tf_op | source)
XLA Modules:
  0.0 57.1 jit_solution(3652666715320845623)
XLA Ops:
  0.6 0.7 %reshape.11.gain_ref = bf16[1,256]{1,0:T(2,128)(2,1)S(1)} reshape(bf16[256]{0:T(256)(128)(2,1)} %param.8) | data formatting | bytes 1024 | tf_op jit(solution)/shard_map/reshape | solution.py:327
  1.3 0.0 copy-start
  1.3 0.9 %copy-done = bf16[512,256]{1,0:T(8,128)(2,1)S(1)} copy-done((bf16[512,256]{1,0:T(8,128)(2,1)S(1)}, bf16[512,256]{1,0:T(8,128)(2,1)}, u32[]{:S(2)}) %copy-start) | copy-done | bytes 262168
  2.2 0.0 copy-start.1
  2.2 0.9 %copy-done.1 = bf16[512,256]{1,0:T(8,128)(2,1)S(1)} copy-done((bf16[512,256]{1,0:T(8,128)(2,1)S(1)}, bf16[512,256]{1,0:T(8,128)(2,1)}, u32[]{:S(2)}) %copy-start.1) | copy-done | bytes 262168
  3.2 0.0 copy-start.2
  3.2 0.9 %copy-done.2 = bf16[512,256]{1,0:T(8,128)(2,1)S(1)} copy-done((bf16[512,256]{1,0:T(8,128)(2,1)S(1)}, bf16[512,256]{1,0:T(8,128)(2,1)}, u32[]{:S(2)}) %copy-start.2) | copy-done | bytes 262168
  4.1 0.0 copy-start.3
  4.1 0.9 %copy-done.3 = bf16[512,256]{1,0:T(8,128)(2,1)S(1)} copy-done((bf16[512,256]{1,0:T(8,128)(2,1)S(1)}, bf16[512,256]{1,0:T(8,128)(2,1)}, u32[]{:S(2)}) %copy-start.3) | copy-done | bytes 262168
  5.1 49.2 %shard_map.84 = (bf16[512,256]{1,0:T(8,128)(2,1)S(1)}, bf16[512,256]{1,0:T(8,128)(2,1)S(1)}, bf16[512,256]{1,0:T(8,128)(2,1)S(1)}, bf16[512,256]{1,0:T(8,128)(2,1)S(1)}) custom-call(bf16[512,256]{1,0:T(8,128)(2,1)S(1)} %copy-done, bf16[512,256]{1,0:T(8,128)(2,1)S(1)} %copy-done.1, bf16[512,256]{1,0:T(8,128)(2,1)S(1)} %copy-done.2, ...), custom_call_target="tpu_custom_call" | custom-call | tf_op jit(solution)/shard_map/pallas_call | solution.py:310
  54.3 0.7 %copy.13 = bf16[512,256]{1,0:T(8,128)(2,1)} copy(bf16[512,256]{1,0:T(8,128)(2,1)S(1)} %get-tuple-element.8) | data formatting | bytes 524288
  55.0 0.7 %copy.14 = bf16[512,256]{1,0:T(8,128)(2,1)} copy(bf16[512,256]{1,0:T(8,128)(2,1)S(1)} %get-tuple-element.9) | data formatting | bytes 524288
  55.7 0.7 %copy.15 = bf16[512,256]{1,0:T(8,128)(2,1)} copy(bf16[512,256]{1,0:T(8,128)(2,1)S(1)} %get-tuple-element.10) | data formatting | bytes 524288
  56.4 0.7 %copy.16 = bf16[512,256]{1,0:T(8,128)(2,1)} copy(bf16[512,256]{1,0:T(8,128)(2,1)S(1)} %get-tuple-element.11) | data formatting | bytes 524288
Async XLA Ops:
  1.3 0.9 %copy-start = (bf16[512,256]{1,0:T(8,128)(2,1)S(1)}, bf16[512,256]{1,0:T(8,128)(2,1)}, u32[]{:S(2)}) copy-start(bf16[512,256]{1,0:T(8,128)(2,1)} %q_in.1) | copy-start | bytes 786436
  2.2 0.9 %copy-start.1 = (bf16[512,256]{1,0:T(8,128)(2,1)S(1)}, bf16[512,256]{1,0:T(8,128)(2,1)}, u32[]{:S(2)}) copy-start(bf16[512,256]{1,0:T(8,128)(2,1)} %k_in.1) | copy-start | bytes 786436
  3.2 0.9 %copy-start.2 = (bf16[512,256]{1,0:T(8,128)(2,1)S(1)}, bf16[512,256]{1,0:T(8,128)(2,1)}, u32[]{:S(2)}) copy-start(bf16[512,256]{1,0:T(8,128)(2,1)} %v_in.1) | copy-start | bytes 786436
  4.1 0.9 %copy-start.3 = (bf16[512,256]{1,0:T(8,128)(2,1)S(1)}, bf16[512,256]{1,0:T(8,128)(2,1)}, u32[]{:S(2)}) copy-start(bf16[512,256]{1,0:T(8,128)(2,1)} %c_in.1) | copy-start | bytes 786436

commit v2 on v1

--- a/solution.py
+++ b/solution.py
@@ -30,11 +30,10 @@
 
 
 def kernel(
-    q_in, k_in, v_in, gain_ref, c_in, n_out, dq_out, dk_out, dv_out,
-    q, k, v, c, scaled, att, grad, m_top, m_low, x_top, x_low, dk_acc, dv_acc,
-    n_buf, dq_buf, dk_buf, dv_buf, prior_bd, after_bd, stats,
+    q_in, k_in, v_in, gain_in, c_in, n_buf, dq_buf, dk_acc, dv_acc, after_bd, k, v,
+    q, c, gain_ref, scaled, att, grad, m_top, m_low, x_top, x_low, prior_bd, stats,
     own_a, gath_a, tot_a, back_a, full_a, own_b, gath_b, tot_b, back_b, full_b,
-    in_sem, out_sem, row_send_a, row_recv_a, col_send_a, col_recv_a, ret_send_a, ret_recv_a,
+    in_sem, row_send_a, row_recv_a, col_send_a, col_recv_a, ret_send_a, ret_recv_a,
     row_send_b, row_recv_b, col_send_b, col_recv_b, ret_send_b, ret_recv_b, tp_send, tp_recv,
 ):
     me = lax.axis_index("ctx")
@@ -44,7 +43,7 @@
 
     loads = [
         pltpu.make_async_copy(src, dst, in_sem.at[i])
-        for i, (src, dst) in enumerate(((k_in, k), (v_in, v), (q_in, q), (c_in, c)))
+        for i, (src, dst) in enumerate(((k_in, k), (v_in, v), (q_in, q), (c_in, c), (gain_in, gain_ref)))
     ]
     for load in loads:
         load.start()
@@ -159,6 +158,7 @@
 
     loads[2].wait()
     loads[3].wait()
+    loads[4].wait()
     lower = lax.broadcasted_iota(jnp.int32, (H, H), 0) >= lax.broadcasted_iota(jnp.int32, (H, H), 1)
 
     def masked_products(left, right, top, low):
@@ -175,7 +175,7 @@
         cols = slice(h * HEAD, (h + 1) * HEAD)
         att[0:H, cols] = dot(m_top[h], v[0:H, cols], 1, 0)
         att[H:T, cols] = dot(m_low[h], v[:, cols], 1, 0)
-    gain = gain_ref[...].astype(F32)
+    gain = jnp.concatenate([gain_ref[h:h + 1, :].astype(F32) for h in range(2)], axis=1)
     scaled[...] = c[...].astype(F32) * gain
 
     received(row_a)
@@ -243,8 +243,6 @@
     for a in range(T // HEAD):
         span = slice(a * HEAD, (a + 1) * HEAD)
         n_buf[span, :] = (att[span, :] * inverse[a] * gain).astype(BF16)
-    stores = [pltpu.make_async_copy(n_buf, n_out, out_sem.at[0])]
-    stores[0].start()
     masked_products(grad, v, x_top, x_low)
 
     received(row_b)
@@ -272,27 +270,31 @@
         from_prior = dot(grad[:, cols], prior_bd[cols, cols], 1, 1)
         dq_buf[0:H, cols] = (dot(x_top[h], k[0:H, cols], 1, 0) + from_prior[0:H]).astype(BF16)
         dq_buf[H:T, cols] = (dot(x_low[h], k[:, cols], 1, 0) + from_prior[H:T]).astype(BF16)
-    stores.append(pltpu.make_async_copy(dq_buf, dq_out, out_sem.at[1]))
-    stores[1].start()
     for copies in (row_a, col_a, ret_a, tp_copies, row_b, col_b):
         sent(copies)
 
     received(ret_b)
     put_bd(after_bd, full_b)
+    sent(ret_b)
+
+
+def last_kernel(n_buf, dq_buf, dk_acc, dv_acc, after_bd, k, v, n_out, dq_out, dk_out, dv_out, dk_buf, dv_buf, out_sem):
+    stores = [
+        pltpu.make_async_copy(src, dst, out_sem.at[i])
+        for i, (src, dst) in enumerate(((n_buf, n_out), (dq_buf, dq_out), (dk_buf, dk_out), (dv_buf, dv_out)))
+    ]
+    stores[0].start()
+    stores[1].start()
     dk_buf[...] = (dk_acc[...] + dot(v[...], after_bd[...], 1, 1)).astype(BF16)
-    stores.append(pltpu.make_async_copy(dk_buf, dk_out, out_sem.at[2]))
     stores[2].start()
     dv_buf[...] = (dv_acc[...] + dot(k[...], after_bd[...], 1, 0)).astype(BF16)
-    stores.append(pltpu.make_async_copy(dv_buf, dv_out, out_sem.at[3]))
     stores[3].start()
-    sent(ret_b)
     for store in stores:
         store.wait()
 
 
 def shards(queries, keys, values, gain, cotangent):
     block = jax.ShapeDtypeStruct((T, W), BF16)
-    anywhere = pl.BlockSpec(memory_space=pl.ANY)
     low = pltpu.VMEM((T, W), BF16)
     wide = pltpu.VMEM((T, W), F32)
     dma = pltpu.SemaphoreType.DMA
@@ -307,24 +309,37 @@
     top = pltpu.VMEM((2, H, H), BF16)
     bottom = pltpu.VMEM((2, H, T), BF16)
     square = pltpu.VMEM((W, W), BF16)
-    return pl.pallas_call(
+    hbm = pl.BlockSpec(memory_space=pltpu.HBM)
+    local = pl.BlockSpec(memory_space=pltpu.VMEM)
+    wide_out = jax.ShapeDtypeStruct((T, W), F32)
+    queries, keys, values, gain, cotangent = (
+        pltpu.with_memory_space_constraint(array, pltpu.HBM)
+        for array in (queries, keys, values, gain.reshape(2, HEAD), cotangent)
+    )
+    kept = pl.pallas_call(
         kernel,
-        out_shape=(block,) * 4,
-        in_specs=[anywhere, anywhere, anywhere, pl.BlockSpec(memory_space=pltpu.VMEM), anywhere],
-        out_specs=(anywhere,) * 4,
-        scratch_shapes=[low, low, low, low, wide, wide, low, top, bottom, top, bottom, wide, wide]
-        + [low] * 4
-        + [square, square, pltpu.VMEM((TP, 8, HEAD), F32)]
+        out_shape=(block, block, wide_out, wide_out, jax.ShapeDtypeStruct((W, W), BF16), block, block),
+        in_specs=[hbm] * 5,
+        out_specs=(local,) * 7,
+        scratch_shapes=[low, low, pltpu.VMEM((2, HEAD), BF16), wide, wide, low, top, bottom, top, bottom, square, pltpu.VMEM((TP, 8, HEAD), F32)]
         + scan_buffers
         + scan_buffers
-        + [dma((4,)), dma((4,))]
+        + [dma((5,))]
         + scan_sems
         + scan_sems
         + [dma((TP,)), dma((TP,))],
         compiler_params=pltpu.CompilerParams(
-            collective_id=0, has_side_effects=True, vmem_limit_bytes=40 * 1024 * 1024
+            collective_id=0, has_side_effects=True, vmem_limit_bytes=32 * 1024 * 1024
         ),
-    )(queries, keys, values, gain.reshape(1, W), cotangent)
+    )(queries, keys, values, gain, cotangent)
+    return pl.pallas_call(
+        last_kernel,
+        out_shape=(block,) * 4,
+        in_specs=[local] * 7,
+        out_specs=(hbm,) * 4,
+        scratch_shapes=[low, low, dma((4,))],
+        compiler_params=pltpu.CompilerParams(vmem_limit_bytes=16 * 1024 * 1024),
+    )(*kept)
 
 
 def solution(mesh):

time: 57.3 us -> 50.3 us (0.88)
  local copies, waits for them, and re-layouts: 7.27 us -> 0 us
    unnamed x12 -> x0, local copies, waits for them, and re-layouts: 6.61 us -> none
    reshape x1 -> x0, local copies, waits for them, and re-layouts: 0.66 us -> none  [shards(): gain.reshape(1, W)]
    pallas_call x1 -> x2, Pallas kernels: 49.2 us -> 49.6 us  [the longest x1 48.4 us: shards(): pl.pallas_call(kernel, out_shape=(block, block, wide_out, wide_out, jax.S...]
where the time goes in v2:
time: 50.3 us; the launch traced here: 50.2 us
  Pallas kernels  49.6 us (99%)
  between operations  0.64 us (1%)
    pallas_call x1, Pallas kernels, shards(): pl.pallas_call(kernel, out_shape=(block, block, wide_out, wide_out, jax.S...  48.4 us
    pallas_call x1, Pallas kernels, shards(): pl.pallas_call(last_kernel, out_shape=(block,) * 4, in_specs=[local] * 7,...  1.15 us

profile of v2, /device:TPU:1, one launch (start us, length us, event | category | flops | bytes accessed | tf_op | source)
XLA Modules:
  0.0 50.2 jit_solution(11136516020124640638)
XLA Ops:
  0.6 48.4 %shard_map.84 = (bf16[512,256]{1,0:T(8,128)(2,1)S(1)}, bf16[512,256]{1,0:T(8,128)(2,1)S(1)}, f32[512,256]{1,0:T(8,128)S(1)}, f32[512,256]{1,0:T(8,128)S(1)}, bf1...) custom-call(bf16[512,256]{1,0:T(8,128)(2,1)} %q_in.1, ...), custom_call_target="tpu_custom_call" | custom-call | tf_op jit(solution)/shard_map/pallas_call | solution.py:319
  49.1 1.1 %shard_map.85 = (bf16[512,256]{1,0:T(8,128)(2,1)}, bf16[512,256]{1,0:T(8,128)(2,1)}, bf16[512,256]{1,0:T(8,128)(2,1)}, bf16[512,256]{1,0:T(8,128)(2,1)}) custom-call(bf16[512,256]{1,0:T(8,128)(2,1)S(1)} %get-tuple-element.11.n_buf, bf16[512,256]{1,0:T(8,128)(2,1)S(1)} %get-tuple-element.12.dq_buf, f32[512,256]{1,0:T(8,128)S(1)} %get-tuple-element.13.dk_acc, ...), custom_call_target="tpu_custom_call" | custom-call | tf_op jit(solution)/shard_map/pallas_call | solution.py:335

commit v3 on v2

v3 whole, which is shorter than its diff:
```python
import jax
import jax.numpy as jnp
from jax import lax
from jax.experimental import pallas as pl
from jax.experimental.pallas import tpu as pltpu
from jax.sharding import PartitionSpec as P

HEAD = 128
HEADS = 16
D = HEAD * HEADS
ROW = 16
COLS = 4
TP = 8
T = 512
H = T // 2
W = 256
CHIPS = 8
PIECE = HEAD // CHIPS
epsilon = 1e-06
F32 = jnp.float32
BF16 = jnp.bfloat16
MESH = pl.DeviceIdType.MESH

RING_ORDER = (4, 3, 5, 2, 6, 1, 7)
COL_ORDER = (2, 1, 3)


def dot(a, b, ca, cb):
    return lax.dot_general(a, b, (((ca,), (cb,)), ((), ())), preferred_element_type=F32)


def kernel(
    q_in, k_in, v_in, gain_in, c_in, n_buf, dq_buf, dk_acc, dv_acc, after_bd, k, v,
    q, c_block, gain_ref, scaled, att, grad, m_top, m_low, x_top, x_low, prior_bd, stats,
    own_a, mate_a, chip_a, gath_a, tot_a, back_a, part_a, mess_a, full_a,
    own_b, mate_b, chip_b, gath_b, tot_b, back_b, part_b, mess_b, full_b,
    in_sem, near_a, far_a, ret_a, col_a, near_b, far_b, ret_b, col_b, tp_send, tp_recv,
):
    me = lax.axis_index("ctx")
    z = lax.axis_index("tp")
    x = me // ROW
    y = (me % ROW) // 2
    c = me % 2

    loads = [
        pltpu.make_async_copy(src, dst, in_sem.at[i])
        for i, (src, dst) in enumerate(((k_in, k), (v_in, v), (q_in, q), (c_in, c_block), (gain_in, gain_ref)))
    ]
    for load in loads:
        load.start()

    mate_peer = (me + 1 - 2 * c, z)

    def y_peer(off):
        return (x * ROW + ((y + off) % CHIPS) * 2 + c, z)

    def x_peer(off):
        return (((x + off) % COLS) * ROW + me % ROW, z)

    def tp_peer(off):
        return (me, (z + off) % TP)

    barrier = pltpu.get_barrier_semaphore()
    peers = [mate_peer]
    peers += [y_peer(off) for off in RING_ORDER]
    peers += [x_peer(off) for off in COL_ORDER]
    peers += [tp_peer(off) for off in RING_ORDER]
    for peer in peers:
        pl.semaphore_signal(barrier, inc=1, device_id=peer, device_id_type=MESH)

    prior_bd[...] = jnp.zeros_like(prior_bd)
    after_bd[...] = jnp.zeros_like(after_bd)

    def put_own(own, left, right):
        state = dot(left, right, 0, 0)
        for h in range(2):
            span = slice(h * HEAD, (h + 1) * HEAD)
            own[h] = state[span, span].reshape(CHIPS, PIECE, HEAD)

    def remote(src, dst, send, recv, peer):
        return pltpu.make_async_remote_copy(
            src_ref=src, dst_ref=dst, send_sem=send, recv_sem=recv, device_id=peer, device_id_type=MESH
        )

    def start(copies):
        for copy in copies:
            copy.start()

    def received(copies):
        for copy in copies:
            copy.wait_recv()

    def sent(copies):
        for copy in copies:
            copy.wait_send()

    class Scan:
        def __init__(self, reverse, own, mate, chip, gath, tot, back, part, message, full, near, far, ret, col):
            self.reverse = reverse
            self.own, self.mate, self.chip, self.gath, self.tot = own, mate, chip, gath, tot
            self.back, self.part, self.message, self.full = back, part, message, full
            self.swap = [remote(own.at[1 - c], mate, near.at[0], near.at[1], mate_peer)]
            self.spread = [
                remote(chip.at[(y + off) % CHIPS], gath.at[y], far.at[0, off], far.at[1, off], y_peer(off))
                for off in RING_ORDER
            ]
            self.across = [
                remote(tot.at[x], tot.at[x], col.at[0, off], col.at[1, off], x_peer(off)) for off in COL_ORDER
            ]
            self.gather = [
                remote(back.at[(y + off) % CHIPS], part.at[y], ret.at[0, off], ret.at[1, off], y_peer(off))
                for off in RING_ORDER
            ]
            self.share = [remote(message, full.at[c], near.at[2], near.at[3], mate_peer)]

        def add_chip(self):
            received(self.swap)
            self.chip[...] = self.own[c] + self.mate[...]
            start(self.spread)
            self.gath[y] = self.chip[y]

        def add_row(self):
            received(self.spread)
            run = jnp.zeros((PIECE, HEAD), F32)
            self.before = [None] * CHIPS
            for j in reversed(range(CHIPS)) if self.reverse else range(CHIPS):
                self.before[j] = run
                run = run + self.gath[j]
            self.tot[x] = run
            start(self.across)

        def add_rows(self):
            received(self.across)
            base = jnp.zeros((PIECE, HEAD), F32)
            for other in range(COLS):
                counts = (other > x) if self.reverse else (other < x)
                base = base + jnp.where(counts, self.tot[other], 0.0)
            for j in range(CHIPS):
                self.back[j] = self.before[j] + base
            start(self.gather)
            self.part[y] = self.back[y]

        def exchange(self):
            received(self.gather)
            first = 1 if self.reverse else 0
            self.message[...] = self.part[...] + jnp.where(c == first, self.own[c], 0.0)
            start(self.share)
            self.full[c] = self.part[...] + jnp.where(c == first, 0.0, self.mate[...])

        def finish(self, block_diagonal):
            received(self.share)
            for h in range(2):
                span = slice(h * HEAD, (h + 1) * HEAD)
                block_diagonal[span, span] = self.full[h].reshape(HEAD, HEAD).astype(BF16)

        def drain(self):
            for copies in (self.swap, self.spread, self.across, self.gather, self.share):
                sent(copies)

    fore = Scan(False, own_a, mate_a, chip_a, gath_a, tot_a, back_a, part_a, mess_a, full_a, near_a, far_a, ret_a, col_a)
    aft = Scan(True, own_b, mate_b, chip_b, gath_b, tot_b, back_b, part_b, mess_b, full_b, near_b, far_b, ret_b, col_b)

    loads[0].wait()
    loads[1].wait()
    put_own(own_a, k[...], v[...])
    pl.semaphore_wait(barrier, len(peers))
    start(fore.swap)

    loads[2].wait()
    loads[3].wait()
    loads[4].wait()
    lower = lax.broadcasted_iota(jnp.int32, (H, H), 0) >= lax.broadcasted_iota(jnp.int32, (H, H), 1)

    def masked_products(left, right, top, low):
        for h in range(2):
            cols = slice(h * HEAD, (h + 1) * HEAD)
            top[h] = jnp.where(lower, dot(left[0:H, cols], right[0:H, cols], 1, 1), 0.0).astype(BF16)
            low[h, :, 0:H] = dot(left[H:T, cols], right[0:H, cols], 1, 1).astype(BF16)
            low[h, :, H:T] = jnp.where(
                lower, dot(left[H:T, cols], right[H:T, cols], 1, 1), 0.0
            ).astype(BF16)

    gain = jnp.concatenate([gain_ref[h:h + 1, :].astype(F32) for h in range(2)], axis=1)
    scaled[...] = c_block[...].astype(F32) * gain
    fore.add_chip()
    masked_products(q, k, m_top, m_low)
    for h in range(2):
        cols = slice(h * HEAD, (h + 1) * HEAD)
        att[0:H, cols] = dot(m_top[h], v[0:H, cols], 1, 0)
        att[H:T, cols] = dot(m_low[h], v[:, cols], 1, 0)
    fore.add_row()
    fore.add_rows()
    fore.exchange()
    fore.finish(prior_bd)
    att[...] += dot(q[...], prior_bd[...], 1, 0)

    eye = lax.broadcasted_iota(jnp.int32, (HEAD, HEAD), 0) == lax.broadcasted_iota(
        jnp.int32, (HEAD, HEAD), 1
    )
    rows = []
    for kind in range(2):
        for a in range(T // HEAD):
            part = att[a * HEAD:(a + 1) * HEAD, :]
            other = part if kind == 0 else scaled[a * HEAD:(a + 1) * HEAD, :]
            product = part * other
            sums = jnp.sum(product[:, 0:HEAD] + product[:, HEAD:W], axis=1, keepdims=True)
            rows.append(jnp.sum(jnp.where(eye, sums, 0.0), axis=0, keepdims=True))
    stats[z] = jnp.concatenate(rows, axis=0)
    tp_copies = [
        pltpu.make_async_remote_copy(
            src_ref=stats.at[z],
            dst_ref=stats.at[z],
            send_sem=tp_send.at[off],
            recv_sem=tp_recv.at[off],
            device_id=tp_peer(off),
            device_id_type=MESH,
        )
        for off in RING_ORDER
    ]
    start(tp_copies)
    received(tp_copies)
    totals = jnp.sum(stats[...], axis=0)
    inverse_row = lax.rsqrt(totals[0:4] / D + epsilon)
    coef_row = inverse_row * inverse_row * inverse_row * (totals[4:8] / D)

    def column(row):
        return jnp.sum(jnp.where(eye, row, 0.0), axis=1, keepdims=True)

    inverse = []
    for a in range(T // HEAD):
        span = slice(a * HEAD, (a + 1) * HEAD)
        inverse.append(column(inverse_row[a:a + 1]))
        coef = column(coef_row[a:a + 1])
        grad[span, :] = (inverse[a] * scaled[span, :] - coef * att[span, :]).astype(BF16)

    put_own(own_b, q[...], grad[...])
    start(aft.swap)

    for a in range(T // HEAD):
        span = slice(a * HEAD, (a + 1) * HEAD)
        n_buf[span, :] = (att[span, :] * inverse[a] * gain).astype(BF16)
    aft.add_chip()
    masked_products(grad, v, x_top, x_low)
    for h in range(2):
        cols = slice(h * HEAD, (h + 1) * HEAD)
        dk_acc[0:H, cols] = dot(x_top[h], q[0:H, cols], 0, 0) + dot(x_low[h, :, 0:H], q[H:T, cols], 0, 0)
        dk_acc[H:T, cols] = dot(x_low[h, :, H:T], q[H:T, cols], 0, 0)
    aft.add_row()
    for h in range(2):
        cols = slice(h * HEAD, (h + 1) * HEAD)
        dv_acc[0:H, cols] = dot(m_top[h], grad[0:H, cols], 0, 0) + dot(
            m_low[h, :, 0:H], grad[H:T, cols], 0, 0
        )
        dv_acc[H:T, cols] = dot(m_low[h, :, H:T], grad[H:T, cols], 0, 0)
    aft.add_rows()
    for h in range(2):
        cols = slice(h * HEAD, (h + 1) * HEAD)
        from_prior = dot(grad[:, cols], prior_bd[cols, cols], 1, 1)
        dq_buf[0:H, cols] = (dot(x_top[h], k[0:H, cols], 1, 0) + from_prior[0:H]).astype(BF16)
        dq_buf[H:T, cols] = (dot(x_low[h], k[:, cols], 1, 0) + from_prior[H:T]).astype(BF16)
    fore.drain()
    sent(tp_copies)
    aft.exchange()
    aft.finish(after_bd)
    aft.drain()


def last_kernel(n_buf, dq_buf, dk_acc, dv_acc, after_bd, k, v, n_out, dq_out, dk_out, dv_out, dk_buf, dv_buf, out_sem):
    stores = [
        pltpu.make_async_copy(src, dst, out_sem.at[i])
        for i, (src, dst) in enumerate(((n_buf, n_out), (dq_buf, dq_out), (dk_buf, dk_out), (dv_buf, dv_out)))
    ]
    stores[0].start()
    stores[1].start()
    dk_buf[...] = (dk_acc[...] + dot(v[...], after_bd[...], 1, 1)).astype(BF16)
    stores[2].start()
    dv_buf[...] = (dv_acc[...] + dot(k[...], after_bd[...], 1, 0)).astype(BF16)
    stores[3].start()
    for store in stores:
        store.wait()


def shards(queries, keys, values, gain, cotangent):
    block = jax.ShapeDtypeStruct((T, W), BF16)
    low = pltpu.VMEM((T, W), BF16)
    wide = pltpu.VMEM((T, W), F32)
    dma = pltpu.SemaphoreType.DMA
    pieces = pltpu.VMEM((CHIPS, PIECE, HEAD), F32)
    both = pltpu.VMEM((2, CHIPS, PIECE, HEAD), F32)
    scan_buffers = [both, pieces, pieces, pieces, pltpu.VMEM((COLS, PIECE, HEAD), F32), pieces, pieces, pieces, both]
    scan_sems = [dma((4,)), dma((2, CHIPS)), dma((2, CHIPS)), dma((2, COLS))]
    top = pltpu.VMEM((2, H, H), BF16)
    bottom = pltpu.VMEM((2, H, T), BF16)
    square = pltpu.VMEM((W, W), BF16)
    hbm = pl.BlockSpec(memory_space=pltpu.HBM)
    local = pl.BlockSpec(memory_space=pltpu.VMEM)
    wide_out = jax.ShapeDtypeStruct((T, W), F32)
    queries, keys, values, gain, cotangent = (
        pltpu.with_memory_space_constraint(array, pltpu.HBM)
        for array in (queries, keys, values, gain.reshape(2, HEAD), cotangent)
    )
    kept = pl.pallas_call(
        kernel,
        out_shape=(block, block, wide_out, wide_out, jax.ShapeDtypeStruct((W, W), BF16), block, block),
        in_specs=[hbm] * 5,
        out_specs=(local,) * 7,
        scratch_shapes=[low, low, pltpu.VMEM((2, HEAD), BF16), wide, wide, low, top, bottom, top, bottom, square, pltpu.VMEM((TP, 8, HEAD), F32)]
        + scan_buffers
        + scan_buffers
        + [dma((5,))]
        + scan_sems
        + scan_sems
        + [dma((TP,)), dma((TP,))],
        compiler_params=pltpu.CompilerParams(
            collective_id=0, has_side_effects=True, vmem_limit_bytes=32 * 1024 * 1024
        ),
    )(queries, keys, values, gain, cotangent)
    return pl.pallas_call(
        last_kernel,
        out_shape=(block,) * 4,
        in_specs=[local] * 7,
        out_specs=(hbm,) * 4,
        scratch_shapes=[low, low, dma((4,))],
        compiler_params=pltpu.CompilerParams(vmem_limit_bytes=16 * 1024 * 1024),
    )(*kept)


def solution(mesh):
    in_specs = (P("ctx", "tp"), P("ctx", "tp"), P("ctx", "tp"), P("tp"), P("ctx", "tp"))
    out_specs = (P("ctx", "tp"), P("ctx", "tp"), P("ctx", "tp"), P("ctx", "tp"))
    return jax.shard_map(shards, mesh=mesh, in_specs=in_specs, out_specs=out_specs, check_vma=False)
```

time: 50.3 us -> 51 us (1.014)
  Pallas kernels: 49.6 us -> 50.2 us
    pallas_call x1, Pallas kernels: 48.4 us -> 49.1 us  [shards(): pl.pallas_call(kernel, out_shape=(block, block, wide_out, wide_out, jax.S...]
where the time goes in v3:
time: 51 us; the launch traced here: 50.9 us
  Pallas kernels  50.2 us (98%)
  between operations  0.64 us (1%)
    pallas_call x1, Pallas kernels, shards(): pl.pallas_call(kernel, out_shape=(block, block, wide_out, wide_out, jax.S...  49.1 us
    pallas_call x1, Pallas kernels, shards(): pl.pallas_call(last_kernel, out_shape=(block,) * 4, in_specs=[local] * 7,...  1.15 us

profile of v3, /device:TPU:1, one launch (start us, length us, event | category | flops | bytes accessed | tf_op | source)
XLA Modules:
  0.0 50.9 jit_solution(7779469503467016565)
XLA Ops:
  0.6 49.1 %shard_map.84 = (bf16[512,256]{1,0:T(8,128)(2,1)S(1)}, bf16[512,256]{1,0:T(8,128)(2,1)S(1)}, f32[512,256]{1,0:T(8,128)S(1)}, f32[512,256]{1,0:T(8,128)S(1)}, bf1...) custom-call(bf16[512,256]{1,0:T(8,128)(2,1)} %q_in.1, ...), custom_call_target="tpu_custom_call" | custom-call | tf_op jit(solution)/shard_map/pallas_call | solution.py:302
  49.7 1.1 %shard_map.85 = (bf16[512,256]{1,0:T(8,128)(2,1)}, bf16[512,256]{1,0:T(8,128)(2,1)}, bf16[512,256]{1,0:T(8,128)(2,1)}, bf16[512,256]{1,0:T(8,128)(2,1)}) custom-call(bf16[512,256]{1,0:T(8,128)(2,1)S(1)} %get-tuple-element.11.n_buf, bf16[512,256]{1,0:T(8,128)(2,1)S(1)} %get-tuple-element.12.dq_buf, f32[512,256]{1,0:T(8,128)S(1)} %get-tuple-element.13.dk_acc, ...), custom_call_target="tpu_custom_call" | custom-call | tf_op jit(solution)/shard_map/pallas_call | solution.py:318
